TPU v7x, 32 devices: a whole 2x2x4 slice. The times are simulated.
32 devices in a mesh: dp: 16 (over z, x, core), tensor: 2 (over y).
Axes of the slice: x: 2, y: 2, z: 4, core: 2. Of those that a mesh axis runs over, the one named last changes fastest.
Arguments:
- inputs: bfloat16 [12288, 768], P('dp'), may hold values from -6 to 6
- clip_ids: int32 [12288], replicated, may hold values from 0 to 11, never falling along the last dimension, each value on 1 to 1500 neighbouring positions
- attn_gain: bfloat16 [768], replicated, may hold values from 0.5 to 1.5
- attn_shift: bfloat16 [768], replicated, may hold values from -1.75 to 1.75
- w_query: bfloat16 [768, 768], P(None, 'tensor'), may hold values from -0.21875 to 0.21875
- query_bias: bfloat16 [768], P('tensor'), may hold values from -1.75 to 1.75
- w_key: bfloat16 [768, 768], P(None, 'tensor'), may hold values from -0.21875 to 0.21875
- w_value: bfloat16 [768, 768], P(None, 'tensor'), may hold values from -0.21875 to 0.21875
- value_bias: bfloat16 [768], P('tensor'), may hold values from -3 to 3
- w_out: bfloat16 [768, 768], P('tensor'), may hold values from -4 to 4
- out_bias: bfloat16 [768], replicated, may hold values from -1.75 to 1.75
- mlp_gain: bfloat16 [768], replicated, may hold values from 0.5 to 1.5
- mlp_shift: bfloat16 [768], replicated, may hold values from -1.75 to 1.75
- w_fc1: bfloat16 [768, 3072], P(None, 'tensor'), may hold values from -0.21875 to 0.21875
- fc1_bias: bfloat16 [3072], P('tensor'), may hold values from -3 to 3
- w_fc2: bfloat16 [3072, 768], P('tensor'), may hold values from -0.109375 to 0.109375
- fc2_bias: bfloat16 [768], replicated, may hold values from -1.75 to 1.75
- cotangent: bfloat16 [12288, 768], P('dp'), may hold values from -6 to 6
Outputs:
- layer_out: bfloat16 [12288, 768], P('dp')
- inputs_grad: float32 [12288, 768], P('dp')
- attn_gain_grad: float32 [768], replicated
- attn_shift_grad: float32 [768], replicated
- w_query_grad: float32 [768, 768], P(None, 'tensor')
- query_bias_grad: float32 [768], P('tensor')
- w_key_grad: float32 [768, 768], P(None, 'tensor')
- w_value_grad: float32 [768, 768], P(None, 'tensor')
- value_bias_grad: float32 [768], P('tensor')
- w_out_grad: float32 [768, 768], P('tensor')
- out_bias_grad: float32 [768], replicated
- mlp_gain_grad: float32 [768], replicated
- mlp_shift_grad: float32 [768], replicated
- w_fc1_grad: float32 [768, 3072], P(None, 'tensor')
- fc1_bias_grad: float32 [3072], P('tensor')
- w_fc2_grad: float32 [3072, 768], P('tensor')
- fc2_bias_grad: float32 [768], replicated
Inputs may be any that keep to these rules, and one draw needn't show every extreme that they name: `clip_ids`: clip numbers never fall along the tokens; each of the 12 clips holds 1 to 1500 consecutive tokens, and one holds exactly 1500.
All inputs are finite; a program needn't handle non-finite values.
Results may differ from a plain program's by a relative error of at most 0.012.
Values may be sent and summed in bfloat16 or wider, within the bound.
A program may use at most 128 MiB of HBM per device.

v0:
```python
import jax
import jax.numpy as jnp
from jax import lax
from jax.sharding import PartitionSpec as P

HEAD_DIM = 64
REACH = 2


def from_behind(block, axis, distance):
    devices = range(lax.axis_size(axis))
    route = [(i - distance, i) for i in devices if i - distance in devices]
    return lax.ppermute(block, axis, route)


def layer_norm(values, gain_row, bias_row):
    middle = jnp.mean(values, axis=-1, keepdims=True)
    centred = values - middle
    spread = jnp.mean(centred * centred, axis=-1, keepdims=True)
    return centred * lax.rsqrt(spread + 1e-05) * gain_row + bias_row


def exact_gelu(values):
    return jax.nn.gelu(values, approximate=False)


def matmul(left, right):
    return jnp.dot(left, right, preferred_element_type=jnp.float32)


def contract_rows(left, right):
    return lax.dot_general(
        left, right, (((0,), (0,)), ((), ())), preferred_element_type=jnp.float32
    )


def contract_cols(left, right):
    return lax.dot_general(
        left, right, (((1,), (1,)), ((), ())), preferred_element_type=jnp.float32
    )


def split_heads(values):
    return values.reshape(values.shape[0], values.shape[1] // HEAD_DIM, HEAD_DIM).transpose(1, 0, 2)


def join_heads(stacked):
    return stacked.transpose(1, 0, 2).reshape(stacked.shape[1], stacked.shape[0] * stacked.shape[2])


def on_device(
    inputs,
    clip_ids,
    attn_gain,
    attn_shift,
    w_query,
    query_bias,
    w_key,
    w_value,
    value_bias,
    w_out,
    out_bias,
    mlp_gain,
    mlp_shift,
    w_fc1,
    fc1_bias,
    w_fc2,
    fc2_bias,
    cotangent,
):
    height = inputs.shape[0]
    devices = lax.axis_size("dp")
    myself = lax.axis_index("dp")
    factor = HEAD_DIM ** (-0.5)
    offsets = list(range(-REACH, REACH + 1))

    def clip_block(offset):
        holder = myself + offset
        begin_at = jnp.clip(holder, 0, devices - 1) * height
        labels = lax.dynamic_slice_in_dim(clip_ids, begin_at, height)
        inside = jnp.logical_and(holder >= 0, holder < devices)
        return jnp.where(inside, labels, -1)

    own_labels = clip_block(0)
    key_labels = jnp.concatenate([clip_block(offset) for offset in offsets])
    allowed = own_labels[:, None] == key_labels[None, :]
    source = inputs.astype(jnp.float32)
    normed_one, norm_one_back = jax.vjp(
        layer_norm, source, attn_gain.astype(jnp.float32), attn_shift.astype(jnp.float32)
    )
    attn_input = normed_one.astype(jnp.bfloat16)
    queries = (matmul(attn_input, w_query) + query_bias.astype(jnp.float32)).astype(jnp.bfloat16)
    keys_own = matmul(attn_input, w_key).astype(jnp.bfloat16)
    values_own = (matmul(attn_input, w_value) + value_bias.astype(jnp.float32)).astype(jnp.bfloat16)
    key_parts = []
    value_parts = []
    for offset in offsets:
        if offset == 0:
            key_parts.append(keys_own)
            value_parts.append(values_own)
        else:
            moved_keys, moved_values = from_behind((keys_own, values_own), "dp", -offset)
            key_parts.append(moved_keys)
            value_parts.append(moved_values)
    query_heads = split_heads(queries)
    key_heads = split_heads(jnp.concatenate(key_parts))
    value_heads = split_heads(jnp.concatenate(value_parts))

    def attend(operands):
        query_one, key_one, value_one = operands
        scores = jnp.where(allowed, contract_cols(query_one, key_one) * factor, -1e30)
        largest = jnp.max(scores, axis=1, keepdims=True)
        expset = jnp.exp(scores - largest)
        totals = jnp.sum(expset, axis=1, keepdims=True)
        weights = (expset / totals).astype(jnp.bfloat16)
        mixed_one = matmul(weights, value_one)
        return (mixed_one.astype(jnp.bfloat16), largest[:, 0] + jnp.log(totals[:, 0]))

    head_out, log_totals = lax.map(attend, (query_heads, key_heads, value_heads))
    attn_mixed = join_heads(head_out)
    attn_total = lax.psum(matmul(attn_mixed, w_out), "tensor") + out_bias.astype(jnp.float32)
    residual = source + attn_total
    normed_two, norm_two_back = jax.vjp(
        layer_norm, residual, mlp_gain.astype(jnp.float32), mlp_shift.astype(jnp.float32)
    )
    mlp_input = normed_two.astype(jnp.bfloat16)
    preact = matmul(mlp_input, w_fc1) + fc1_bias.astype(jnp.float32)
    activated_full, gelu_back = jax.vjp(exact_gelu, preact)
    activated = activated_full.astype(jnp.bfloat16)
    mlp_total = lax.psum(matmul(activated, w_fc2).astype(jnp.bfloat16), "tensor").astype(
        jnp.float32
    ) + fc2_bias.astype(jnp.float32)
    layer_out = (residual + mlp_total).astype(jnp.bfloat16)
    out_grad_full = cotangent.astype(jnp.float32)
    fc2_bias_grad = jnp.sum(out_grad_full, axis=0)
    w_fc2_grad = contract_rows(activated, cotangent)
    (pre_full,) = gelu_back(contract_cols(cotangent, w_fc2))
    pre_grad = pre_full.astype(jnp.bfloat16)
    fc1_bias_grad = jnp.sum(pre_grad.astype(jnp.float32), axis=0)
    w_fc1_grad = contract_rows(mlp_input, pre_grad)
    mlp_in_grad = lax.psum(contract_cols(pre_grad, w_fc1), "tensor")
    resid_back, mlp_gain_grad, mlp_shift_grad = norm_two_back(mlp_in_grad)
    residual_grad = out_grad_full + resid_back
    attn_grad_low = residual_grad.astype(jnp.bfloat16)
    out_bias_grad = jnp.sum(attn_grad_low.astype(jnp.float32), axis=0)
    w_out_grad = contract_rows(attn_mixed, attn_grad_low)
    mixed_heads = split_heads(contract_cols(attn_grad_low, w_out).astype(jnp.bfloat16))

    def attend_back(operands):
        query_one, key_one, value_one, log_total, mixed_one = operands
        scores = jnp.where(allowed, contract_cols(query_one, key_one) * factor, -1e30)
        probs = jnp.exp(scores - log_total[:, None])
        probs_low = probs.astype(jnp.bfloat16)
        prob_grad = contract_cols(mixed_one, value_one)
        centre = jnp.sum(probs * prob_grad, axis=1, keepdims=True)
        score_grad = (probs * (prob_grad - centre)).astype(jnp.bfloat16)
        query_part = (matmul(score_grad, key_one) * factor).astype(jnp.bfloat16)
        key_part = contract_rows(score_grad, query_one) * factor
        value_part = contract_rows(probs_low, mixed_one)
        return (query_part, key_part, value_part)

    query_parts, key_grads, value_grads = lax.map(
        attend_back, (query_heads, key_heads, value_heads, log_totals, mixed_heads)
    )
    query_low = join_heads(query_parts)
    key_window_grad = join_heads(key_grads)
    value_window_grad = join_heads(value_grads)
    centre_row = REACH * height
    key_sum = key_window_grad[centre_row : centre_row + height]
    value_sum = value_window_grad[centre_row : centre_row + height]
    for position, offset in enumerate(offsets):
        if offset != 0:
            begin_row = position * height
            back_keys, back_values = (
                from_behind(
                    key_window_grad[begin_row : begin_row + height].astype(jnp.bfloat16),
                    "dp",
                    offset,
                ).astype(jnp.float32),
                from_behind(
                    value_window_grad[begin_row : begin_row + height].astype(jnp.bfloat16),
                    "dp",
                    offset,
                ).astype(jnp.float32),
            )
            key_sum = key_sum + back_keys
            value_sum = value_sum + back_values
    key_low = key_sum.astype(jnp.bfloat16)
    value_low = value_sum.astype(jnp.bfloat16)
    query_bias_grad = jnp.sum(query_low.astype(jnp.float32), axis=0)
    value_bias_grad = jnp.sum(value_low.astype(jnp.float32), axis=0)
    w_query_grad = contract_rows(attn_input, query_low)
    w_key_grad = contract_rows(attn_input, key_low)
    w_value_grad = contract_rows(attn_input, value_low)
    attn_in_part = (
        contract_cols(query_low, w_query)
        + contract_cols(key_low, w_key)
        + contract_cols(value_low, w_value)
    )
    attn_in_grad = lax.psum(attn_in_part.astype(jnp.bfloat16), "tensor").astype(jnp.float32)
    source_back, attn_gain_grad, attn_shift_grad = norm_one_back(attn_in_grad)
    inputs_grad = residual_grad + source_back
    (
        w_query_grad,
        query_bias_grad,
        w_key_grad,
        w_value_grad,
        value_bias_grad,
        w_out_grad,
        out_bias_grad,
        attn_gain_grad,
        attn_shift_grad,
        w_fc1_grad,
        fc1_bias_grad,
        w_fc2_grad,
        fc2_bias_grad,
        mlp_gain_grad,
        mlp_shift_grad,
    ) = lax.psum(
        (
            w_query_grad,
            query_bias_grad,
            w_key_grad,
            w_value_grad,
            value_bias_grad,
            w_out_grad,
            out_bias_grad,
            attn_gain_grad,
            attn_shift_grad,
            w_fc1_grad,
            fc1_bias_grad,
            w_fc2_grad,
            fc2_bias_grad,
            mlp_gain_grad,
            mlp_shift_grad,
        ),
        "dp",
    )
    return (
        layer_out,
        inputs_grad,
        attn_gain_grad,
        attn_shift_grad,
        w_query_grad,
        query_bias_grad,
        w_key_grad,
        w_value_grad,
        value_bias_grad,
        w_out_grad,
        out_bias_grad,
        mlp_gain_grad,
        mlp_shift_grad,
        w_fc1_grad,
        fc1_bias_grad,
        w_fc2_grad,
        fc2_bias_grad,
    )


def solution(mesh):
    in_specs = (
        P("dp", None),
        P(),
        P(),
        P(),
        P(None, "tensor"),
        P("tensor"),
        P(None, "tensor"),
        P(None, "tensor"),
        P("tensor"),
        P("tensor", None),
        P(),
        P(),
        P(),
        P(None, "tensor"),
        P("tensor"),
        P("tensor", None),
        P(),
        P("dp", None),
    )
    out_specs = (
        P("dp", None),
        P("dp", None),
        P(),
        P(),
        P(None, "tensor"),
        P("tensor"),
        P(None, "tensor"),
        P(None, "tensor"),
        P("tensor"),
        P("tensor", None),
        P(),
        P(),
        P(),
        P(None, "tensor"),
        P("tensor"),
        P("tensor", None),
        P(),
    )
    return jax.shard_map(
        on_device, mesh=mesh, in_specs=in_specs, out_specs=out_specs, check_vma=False
    )
```

profile of v0, /device:TPU:0, one launch (start us, length us, event | category | flops | bytes accessed | tf_op | source)
XLA Modules:
  0.0 940.8 jit_solution(11370151416153895606)
XLA Ops:
  15.0 5.8 collective-permute-start
  27.3 6.1 collective-permute-start.4
  44.1 8.9 collective-permute-done
  72.3 6.5 copy.42
  94.9 6.5 copy.43
  102.2 65.1 %while.28 = (s32[]{:T(128)}, bf16[6,768,64]{1,2,0:T(8,128)(2,1)}, f32[6,768]{1,0:T(8,128)}, bf16[6,768,64]{2,1,0:T(8,128)(2,1)}, bf16[6,3840,64]{2,1,0:T(8,128)(...) while((s32[]{:T(128)}, bf16[6,768,64]{1,2,0:T(8,128)(2,1)}, ...), condition=%wide.region_5.6_spmd.clone, body=%wide.region_2.5_spmd.clone.sunk | while | flops 781565184 | bytes 37708912 | solution.py:119
  173.6 80.6 %all-reduce.8.cloned.1.call-done = f32[768,768]{1,0:T(8,128)} async-done(((f32[768,768]{1,0:T(8,128)}), f32[768,768]{1,0:T(8,128)}) %all-reduce.8.cloned.1.call-update) | async-done | bytes 2359312 | tf_op jit(solution)/shard_map/psum | solution.py:121
  261.1 14.3 %convert_reduce_fusion = (f32[1536]{0:T(1024)}, bf16[768,1536]{1,0:T(8,128)(2,1)S(1)}, f32[768,1536]{1,0:T(8,128)}) fusion(f32[768,1536]{1,0:T(8,128)S(1)} %fusion.82, f32[1536]{0:T(1024)S(1)} %copy-done.53, bf16[768,768]{1,0:T(8,128)(2,1)S(1)} %copy-done.18, bf16[1536,768]{1,0:T(8,128)(2,1)S(1)} %copy-done), kind=kOutput, calls=%fused_computation.56 | convolution fusion | flops 1900411392 | bytes 15347712 | tf_op jit(solution)/shard_map/dot_general | solution.py:38
  280.3 4.9 multiply_convert_fusion.1
  289.6 59.4 %all-reduce.10.cloned.1.call-done = f32[768,768]{1,0:T(8,128)} async-done(((f32[768,768]{1,0:T(8,128)}), f32[768,768]{1,0:T(8,128)}) %all-reduce.10.cloned.1.call-update) | async-done | bytes 2359312 | tf_op jit(solution)/shard_map/psum | solution.py:141
  357.3 137.6 %while.29 = (s32[]{:T(128)}, bf16[6,768,64]{1,2,0:T(8,128)(2,1)S(1)}, f32[6,3840,64]{1,2,0:T(8,128)}, f32[6,3840,64]{1,2,0:T(8,128)}, bf16[6,768,64]{2,1,0:T(8,1...) while((s32[]{:T(128)}, ...), condition=%wide.region_15.16_spmd.clone, body=%wide.region_13.15_spmd.clone.sunk | while | flops 1917271296 | bytes 117906592 | solution.py:162
  361.0 5.0 multiply_reduce_fusion.5
  370.0 5.0 fusion.165
  383.9 5.0 multiply_reduce_fusion.5
  392.9 5.0 fusion.165
  406.9 5.0 multiply_reduce_fusion.5
  415.9 5.0 fusion.165
  429.8 5.0 multiply_reduce_fusion.5
  438.8 5.0 fusion.165
  452.7 5.0 multiply_reduce_fusion.5
  461.7 5.0 fusion.165
  475.6 5.0 multiply_reduce_fusion.5
  484.6 5.0 fusion.165
  496.5 5.1 bitcast_convert_fusion
  509.6 6.9 collective-permute-start.15
  518.8 19.1 %collective-permute-done.11 = bf16[768,384]{0,1:T(8,128)(2,1)S(1)} collective-permute-done((bf16[768,384]{0,1:T(8,128)(2,1)S(1)}, bf16[768,384]{0,1:T(8,128)(2,1)S(1)}, u32[]{:S(2)}, u32[]{:S(2)}) %collective-permute-start.11) | collective-permute-done | bytes 589856 | tf_op jit(solution)/shard_map/ppermute | solution.py:13
  543.3 13.5 %collective-permute-done.15 = bf16[768,384]{0,1:T(8,128)(2,1)S(1)} collective-permute-done((bf16[768,384]{0,1:T(8,128)(2,1)S(1)}, bf16[768,384]{0,1:T(8,128)(2,1)S(1)}, u32[]{:S(2)}, u32[]{:S(2)}) %collective-permute-start.15) | collective-permute-done | bytes 589856 | tf_op jit(solution)/shard_map/ppermute | solution.py:13
  558.0 21.4 %collective-permute-done.12 = bf16[768,384]{0,1:T(8,128)(2,1)S(1)} collective-permute-done((bf16[768,384]{0,1:T(8,128)(2,1)S(1)}, bf16[768,384]{0,1:T(8,128)(2,1)S(1)}, u32[]{:S(2)}, u32[]{:S(2)}) %collective-permute-start.12) | collective-permute-done | bytes 589856 | tf_op jit(solution)/shard_map/ppermute | solution.py:13
  582.5 6.4 fusion.99
  605.3 48.7 %all-reduce.14.cloned.1.call-done = (bf16[768,768]{1,0:T(8,128)(2,1)}, bf16[768,768]{1,0:T(8,128)(2,1)}) async-done(((bf16[768,768]{1,0:T(8,128)(2,1)}, bf16[768,768]{1,0:T(8,128)(2,1)}), (bf16[768,768]{1,0:T(8,128)(2,1)}, bf16[768,768]{1,0:T(8,128)(2,1)})) %all-reduce.14.cloned.1.call-update) | async-done | bytes 2359312 | tf_op jit(solution)/shard_map/psum | solution.py:130
  661.7 65.9 %all-reduce = (f32[768]{0:T(1024)}, f32[768]{0:T(1024)}, f32[384]{0:T(512)}, f32[384]{0:T(512)}, f32[768]{0:T(1024)}, /*index=5*/f32[768]{0:T(1024)}, f32[768]{0:T(1024)}, f32[1536]{0:T(1024)}, f32[768]{0:T(1024)}) all-reduce(f32[768]{0:T(1024)} %get-tuple-element.181, ...), channel_id=1, replica_groups=mesh['dp'=16,'tensor'=2] {'dp'}, use_global_device_ids=true, to_apply=%region_20.21 | all-reduce | flops 6912 | bytes 55296 | tf_op jit(solution)/shard_map/psum | solution.py:219
  730.3 191.6 %all-reduce.12.cloned.1.call-done = (f32[768,384]{1,0:T(8,128)}, f32[768,384]{1,0:T(8,128)}, f32[768,384]{1,0:T(8,128)}, f32[384,768]{1,0:T(8,128)}, f32[768,1536]{1,0:T(8,128)}, /*index=5*/f32[1536,768]{1,0:T(8,128)}) async-done(((f32[768,384]{1,0:T(8,128)}, f32[768,384]{1,0:T(8,128)}, f32[768,384]{1,0:T(8,128)}, f32[384,768]{1,0:T(8,128)}, f32[768,1536]{1,0:T(8,128)}, /*index=5*/f32[1536,768]{1,0:T(8,128)}), ...) | async-done | bytes 14155792 | tf_op jit(solution)/shard_map/psum | solution.py:219
  (326 shorter events, 294.3 us)
Async XLA Ops:
  7.2 253.9 %copy-start = (bf16[1536,768]{1,0:T(8,128)(2,1)S(1)}, bf16[1536,768]{1,0:T(8,128)(2,1)}, u32[]{:S(2)}) copy-start(bf16[1536,768]{1,0:T(8,128)(2,1)} %param.37) | copy-start | bytes 7077892
  7.2 247.1 %all-reduce.8.cloned.1.call-start = ((), (), s32[]{:S(2)}) async-start(), calls=%async_computation | async-start | bytes 4718592 | tf_op jit(solution)/shard_map/psum | solution.py:121
  15.0 38.0 %collective-permute-start = (bf16[768,384]{1,0:T(8,128)(2,1)}, bf16[768,384]{1,0:T(8,128)(2,1)}, u32[]{:S(2)}, u32[]{:S(2)}) collective-permute-start(bf16[768,384]{1,0:T(8,128)(2,1)} %convolution_convert_fusion.2), channel_id=1, source_target_pairs={{0,4},{2,6},{4,8},{6,10},{8,12},{10,14},{12,16},{14,18},{16,20},{1... | collective-permute-start | bytes 1769480 | tf_op jit(solution)/shard_map/ppermute | solution.py:13
  20.8 36.2 %collective-permute-start.1 = (bf16[768,384]{1,0:T(8,128)(2,1)}, bf16[768,384]{1,0:T(8,128)(2,1)}, u32[]{:S(2)}, u32[]{:S(2)}) collective-permute-start(bf16[768,384]{1,0:T(8,128)(2,1)} %convolution_convert_fusion.2), channel_id=1, source_target_pairs={{0,2},{2,4},{4,6},{6,8},{8,10},{10,12},{12,14},{14,16},{16,18},{18... | collective-permute-start | bytes 1769480 | tf_op jit(solution)/shard_map/ppermute | solution.py:13
  23.1 39.1 %collective-permute-start.2 = (bf16[768,384]{1,0:T(8,128)(2,1)}, bf16[768,384]{1,0:T(8,128)(2,1)}, u32[]{:S(2)}, u32[]{:S(2)}) collective-permute-start(bf16[768,384]{1,0:T(8,128)(2,1)} %convolution_convert_fusion.2), channel_id=1, source_target_pairs={{2,0},{4,2},{6,4},{8,6},{10,8},{12,10},{14,12},{16,14},{18,16},{20... | collective-permute-start | bytes 1769480 | tf_op jit(solution)/shard_map/ppermute | solution.py:13
  24.4 41.5 %collective-permute-start.3 = (bf16[768,384]{1,0:T(8,128)(2,1)}, bf16[768,384]{1,0:T(8,128)(2,1)}, u32[]{:S(2)}, u32[]{:S(2)}) collective-permute-start(bf16[768,384]{1,0:T(8,128)(2,1)} %convolution_convert_fusion.2), channel_id=1, source_target_pairs={{4,0},{6,2},{8,4},{10,6},{12,8},{14,10},{16,12},{18,14},{20,16},{2... | collective-permute-start | bytes 1769480 | tf_op jit(solution)/shard_map/ppermute | solution.py:13
  27.3 51.5 %collective-permute-start.4 = (bf16[768,384]{1,0:T(8,128)(2,1)}, bf16[768,384]{1,0:T(8,128)(2,1)}, u32[]{:S(2)}, u32[]{:S(2)}) collective-permute-start(bf16[768,384]{1,0:T(8,128)(2,1)} %fusion.70), channel_id=1, source_target_pairs={{0,4},{2,6},{4,8},{6,10},{8,12},{10,14},{12,16},{14,18},{16,20},{1... | collective-permute-start | bytes 1769480 | tf_op jit(solution)/shard_map/ppermute | solution.py:13
  53.0 27.8 %collective-permute-start.5 = (bf16[768,384]{1,0:T(8,128)(2,1)}, bf16[768,384]{1,0:T(8,128)(2,1)}, u32[]{:S(2)}, u32[]{:S(2)}) collective-permute-start(bf16[768,384]{1,0:T(8,128)(2,1)} %fusion.70), channel_id=1, source_target_pairs={{0,2},{2,4},{4,6},{6,8},{8,10},{10,12},{12,14},{14,16},{16,18},{18... | collective-permute-start | bytes 1769480 | tf_op jit(solution)/shard_map/ppermute | solution.py:13
  57.0 27.6 %collective-permute-start.6 = (bf16[768,384]{1,0:T(8,128)(2,1)}, bf16[768,384]{1,0:T(8,128)(2,1)}, u32[]{:S(2)}, u32[]{:S(2)}) collective-permute-start(bf16[768,384]{1,0:T(8,128)(2,1)} %fusion.70), channel_id=1, source_target_pairs={{2,0},{4,2},{6,4},{8,6},{10,8},{12,10},{14,12},{16,14},{18,16},{20... | collective-permute-start | bytes 1769480 | tf_op jit(solution)/shard_map/ppermute | solution.py:13
  62.2 26.3 %collective-permute-start.7 = (bf16[768,384]{1,0:T(8,128)(2,1)}, bf16[768,384]{1,0:T(8,128)(2,1)}, u32[]{:S(2)}, u32[]{:S(2)}) collective-permute-start(bf16[768,384]{1,0:T(8,128)(2,1)} %fusion.70), channel_id=1, source_target_pairs={{4,0},{6,2},{8,4},{10,6},{12,8},{14,10},{16,12},{18,14},{20,16},{2... | collective-permute-start | bytes 1769480 | tf_op jit(solution)/shard_map/ppermute | solution.py:13
  170.8 178.2 %all-reduce.10.cloned.1.call-start = ((), (), s32[]{:S(2)}) async-start(), calls=%async_computation.1 | async-start | bytes 4718592 | tf_op jit(solution)/shard_map/psum | solution.py:141
  173.0 180.0 %copy-start.45 = (f32[768]{0:T(1024)}, f32[768]{0:T(1024)S(1)}, u32[]{:S(2)}) copy-start(f32[768]{0:T(1024)S(1)} %convert_element_type.175) | copy-start | bytes 9220
  256.4 96.6 %copy-start.41 = (f32[768]{0:T(1024)}, f32[768]{0:T(1024)S(1)}, u32[]{:S(2)}) copy-start(f32[768]{0:T(1024)S(1)} %broadcast_multiply_fusion) | copy-start | bytes 9220
  258.9 94.1 %copy-start.47 = (f32[768]{0:T(1024)}, f32[768]{0:T(1024)S(1)}, u32[]{:S(2)}) copy-start(f32[768]{0:T(1024)S(1)} %fusion.80) | copy-start | bytes 9220
  280.2 373.7 %all-reduce.14.cloned.1.call-start = ((), (), s32[]{:S(2)}) async-start(), calls=%async_computation.3 | async-start | bytes 4718592 | tf_op jit(solution)/shard_map/psum | solution.py:130
  289.6 63.4 %copy-start.4 = (f32[768,768]{1,0:T(8,128)S(1)}, f32[768,768]{1,0:T(8,128)}, u32[]{:S(2)}) copy-start(f32[768,768]{1,0:T(8,128)} %copy-done.3) | copy-start | bytes 7077892
  494.9 98.6 %copy-start.14 = (bf16[6,768,64]{1,2,0:T(8,128)(2,1)}, bf16[6,768,64]{1,2,0:T(8,128)(2,1)S(1)}, u32[]{:S(2)}) copy-start(bf16[6,768,64]{1,2,0:T(8,128)(2,1)S(1)} %get-tuple-element.111) | copy-start | bytes 1769476
  501.8 36.1 %collective-permute-start.11 = (bf16[768,384]{0,1:T(8,128)(2,1)S(1)}, bf16[768,384]{0,1:T(8,128)(2,1)S(1)}, u32[]{:S(2)}, u32[]{:S(2)}) collective-permute-start(bf16[768,384]{0,1:T(8,128)(2,1)S(1)} %bitcast.188), channel_id=1, source_target_pairs={{0,4},{2,6},{4,8},{6,10},{8,12},{10,14},{12,16},{14,18},{16,20},{1... | collective-permute-start | bytes 1769480 | tf_op jit(solution)/shard_map/ppermute | solution.py:13
  505.2 34.0 %collective-permute-start.10 = (bf16[768,384]{0,1:T(8,128)(2,1)S(1)}, bf16[768,384]{0,1:T(8,128)(2,1)S(1)}, u32[]{:S(2)}, u32[]{:S(2)}) collective-permute-start(bf16[768,384]{0,1:T(8,128)(2,1)S(1)} %bitcast.187), channel_id=1, source_target_pairs={{0,2},{2,4},{4,6},{6,8},{8,10},{10,12},{12,14},{14,16},{16,18},{18... | collective-permute-start | bytes 1769480 | tf_op jit(solution)/shard_map/ppermute | solution.py:13
  506.7 33.8 %collective-permute-start.9 = (bf16[768,384]{0,1:T(8,128)(2,1)S(1)}, bf16[768,384]{0,1:T(8,128)(2,1)S(1)}, u32[]{:S(2)}, u32[]{:S(2)}) collective-permute-start(bf16[768,384]{0,1:T(8,128)(2,1)S(1)} %bitcast.185), channel_id=1, source_target_pairs={{2,0},{4,2},{6,4},{8,6},{10,8},{12,10},{14,12},{16,14},{18,16},{20... | collective-permute-start | bytes 1769480 | tf_op jit(solution)/shard_map/ppermute | solution.py:13
  508.0 34.0 %collective-permute-start.8 = (bf16[768,384]{0,1:T(8,128)(2,1)S(1)}, bf16[768,384]{0,1:T(8,128)(2,1)S(1)}, u32[]{:S(2)}, u32[]{:S(2)}) collective-permute-start(bf16[768,384]{0,1:T(8,128)(2,1)S(1)} %bitcast.181), channel_id=1, source_target_pairs={{4,0},{6,2},{8,4},{10,6},{12,8},{14,10},{16,12},{18,14},{20,16},{2... | collective-permute-start | bytes 1769480 | tf_op jit(solution)/shard_map/ppermute | solution.py:13
  509.6 47.2 %collective-permute-start.15 = (bf16[768,384]{0,1:T(8,128)(2,1)S(1)}, bf16[768,384]{0,1:T(8,128)(2,1)S(1)}, u32[]{:S(2)}, u32[]{:S(2)}) collective-permute-start(bf16[768,384]{0,1:T(8,128)(2,1)S(1)} %bitcast.186), channel_id=1, source_target_pairs={{0,4},{2,6},{4,8},{6,10},{8,12},{10,14},{12,16},{14,18},{16,20},{1... | collective-permute-start | bytes 1769480 | tf_op jit(solution)/shard_map/ppermute | solution.py:13
  537.9 19.0 %collective-permute-start.14 = (bf16[768,384]{0,1:T(8,128)(2,1)S(1)}, bf16[768,384]{0,1:T(8,128)(2,1)S(1)}, u32[]{:S(2)}, u32[]{:S(2)}) collective-permute-start(bf16[768,384]{0,1:T(8,128)(2,1)S(1)} %bitcast.184), channel_id=1, source_target_pairs={{0,2},{2,4},{4,6},{6,8},{8,10},{10,12},{12,14},{14,16},{16,18},{18... | collective-permute-start | bytes 1769480 | tf_op jit(solution)/shard_map/ppermute | solution.py:13
  539.2 18.8 %collective-permute-start.13 = (bf16[768,384]{0,1:T(8,128)(2,1)S(1)}, bf16[768,384]{0,1:T(8,128)(2,1)S(1)}, u32[]{:S(2)}, u32[]{:S(2)}) collective-permute-start(bf16[768,384]{0,1:T(8,128)(2,1)S(1)} %bitcast.183), channel_id=1, source_target_pairs={{2,0},{4,2},{6,4},{8,6},{10,8},{12,10},{14,12},{16,14},{18,16},{20... | collective-permute-start | bytes 1769480 | tf_op jit(solution)/shard_map/ppermute | solution.py:13
  540.5 38.9 %collective-permute-start.12 = (bf16[768,384]{0,1:T(8,128)(2,1)S(1)}, bf16[768,384]{0,1:T(8,128)(2,1)S(1)}, u32[]{:S(2)}, u32[]{:S(2)}) collective-permute-start(bf16[768,384]{0,1:T(8,128)(2,1)S(1)} %bitcast.182), channel_id=1, source_target_pairs={{4,0},{6,2},{8,4},{10,6},{12,8},{14,10},{16,12},{18,14},{20,16},{2... | collective-permute-start | bytes 1769480 | tf_op jit(solution)/shard_map/ppermute | solution.py:13
  543.3 37.2 %copy-start.29 = (bf16[768,384]{1,0:T(8,128)(2,1)S(1)}, bf16[768,384]{1,0:T(8,128)(2,1)}, u32[]{:S(2)}) copy-start(bf16[768,384]{1,0:T(8,128)(2,1)} %param.29) | copy-start | bytes 1769476
  582.5 339.4 %all-reduce.12.cloned.1.call-start = ((), (), s32[]{:S(2)}) async-start(), calls=%async_computation.2 | async-start | bytes 28311552 | tf_op jit(solution)/shard_map/psum | solution.py:219
  600.7 53.2 %copy-start.7 = (bf16[768,768]{1,0:T(8,128)(2,1)S(1)}, bf16[768,768]{1,0:T(8,128)(2,1)}, u32[]{:S(2)}) copy-start(bf16[768,768]{1,0:T(8,128)(2,1)} %param.22) | copy-start | bytes 3538948
  600.7 53.2 %copy-start.36 = (f32[768]{0:T(1024)S(1)}, f32[768]{0:T(1024)}, u32[]{:S(2)}) copy-start(f32[768]{0:T(1024)} %copy-done.35) | copy-start | bytes 9220
  600.7 53.2 %copy-start.38 = (f32[768]{0:T(1024)S(1)}, f32[768]{0:T(1024)}, u32[]{:S(2)}) copy-start(f32[768]{0:T(1024)} %copy-done.37) | copy-start | bytes 9220
  600.7 56.1 %copy-start.50 = (f32[768]{0:T(1024)S(1)}, f32[768]{0:T(1024)}, u32[]{:S(2)}) copy-start(f32[768]{0:T(1024)} %copy-done.49) | copy-start | bytes 9220
  600.8 56.1 %copy-start.40 = (f32[768]{0:T(1024)S(1)}, f32[768]{0:T(1024)}, u32[]{:S(2)}) copy-start(f32[768]{0:T(1024)} %copy-done.39) | copy-start | bytes 9220
  (59 other events, 329.8 us)
Sparse Core Ops, SparseCore 0:
  171.0 83.2 all-reduce.7
  280.3 68.6 all-reduce.9
  582.5 71.3 all-reduce.13
  660.9 260.8 all-reduce.11
where the time goes:
time: 949 us; the launch traced here: 941 us
  waiting for transfers between devices  446 us (47%)
  matrix products  208 us (22%)
  other arithmetic  82.8 us (9%)
  local copies, waits for them, and re-layouts  81.3 us (9%)
  blocking collectives  65.9 us (7%)
  starting transfers between devices  40.8 us (4%)
  between operations  15 us (2%)
    psum x1, waiting for transfers between devices, on_device(): lax.psum((w_query_grad, query_bias_grad, w_key_grad, w_value_grad, value_...  192 us
    dot_general x24, matrix products, contract_cols(): lax.dot_general(left, right, (((1,), (1,)), ((), ())), preferred_element_...  88.8 us
    psum x1, waiting for transfers between devices, on_device(): lax.psum(matmul(attn_mixed, w_out), 'tensor') + out_bias.astype(jnp.float32)  80.6 us
    dot_general x18, matrix products, matmul(): return jnp.dot(left, right, preferred_element_type=jnp.float32)  69.8 us
    ppermute x16, waiting for transfers between devices, from_behind(): return lax.ppermute(block, axis, route)  66 us
    psum x1, blocking collectives, on_device(): lax.psum((w_query_grad, query_bias_grad, w_key_grad, w_value_grad, value_...  65.9 us
    psum x1, waiting for transfers between devices, on_device(): mlp_in_grad = lax.psum(contract_cols(pre_grad, w_fc1), 'tensor')  59.4 us
    dot_general x18, matrix products, contract_rows(): lax.dot_general(left, right, (((0,), (0,)), ((), ())), preferred_element_...  49.8 us
  transfers between devices with their start and end apart: 20, of which 10 were waited for; matrix products, arithmetic and copies ran while one was open for 9% of the time, Pallas kernels for 0%

commit v1 on v0

--- a/solution.py
+++ b/solution.py
@@ -127,9 +127,9 @@
     preact = matmul(mlp_input, w_fc1) + fc1_bias.astype(jnp.float32)
     activated_full, gelu_back = jax.vjp(exact_gelu, preact)
     activated = activated_full.astype(jnp.bfloat16)
-    mlp_total = lax.psum(matmul(activated, w_fc2).astype(jnp.bfloat16), "tensor").astype(
-        jnp.float32
-    ) + fc2_bias.astype(jnp.float32)
+    mlp_total = jnp.sum(
+        lax.all_gather(matmul(activated, w_fc2).astype(jnp.bfloat16), "tensor"), axis=0
+    ).astype(jnp.float32) + fc2_bias.astype(jnp.float32)
     layer_out = (residual + mlp_total).astype(jnp.bfloat16)
     out_grad_full = cotangent.astype(jnp.float32)
     fc2_bias_grad = jnp.sum(out_grad_full, axis=0)

time: 949 us -> 998 us (1.052)
  matrix products: 208 us -> 229 us
  local copies, waits for them, and re-layouts: 81.3 us -> 95.9 us
  waiting for transfers between devices: 446 us -> 456 us
    all_gather x0 -> x1, waiting for transfers between devices: none -> 34.5 us  [on_device(): lax.all_gather(matmul(activated, w_fc2).astype(jnp.bfloat16), 'tensor')]
    while x12 -> x24, local copies, waits for them, and re-layouts: 0.02 us -> 15.5 us
    dot_general x18, matrix products: 49.8 us -> 62.4 us  [contract_rows(): lax.dot_general(left, right, (((0,), (0,)), ((), ())), preferred_element_...]
    psum x1, waiting for transfers between devices: 48.7 us -> 36.1 us  [on_device(): lax.psum(attn_in_part.astype(jnp.bfloat16), 'tensor').astype(jnp.float32)]
    psum x1, waiting for transfers between devices: 59.4 us -> 47.4 us  [on_device(): mlp_in_grad = lax.psum(contract_cols(pre_grad, w_fc1), 'tensor')]
    unnamed x146 -> x124, local copies, waits for them, and re-layouts: 46.8 us -> 46.9 us
  transfers between devices with their start and end apart: 20 -> 21, of which waited for: 10 -> 9; matrix products, arithmetic and copies ran while one was open for 9% -> 9% of each run, Pallas kernels for 0% -> 0%
where the time goes in v1:
time: 998 us; the launch traced here: 990 us
  waiting for transfers between devices  456 us (46%)
  matrix products  229 us (23%)
  local copies, waits for them, and re-layouts  95.9 us (10%)
  other arithmetic  84.9 us (9%)
  blocking collectives  65.9 us (7%)
  starting transfers between devices  43 us (4%)
  between operations  15 us (2%)
    psum x1, waiting for transfers between devices, on_device(): lax.psum((w_query_grad, query_bias_grad, w_key_grad, w_value_grad, value_...  192 us
    dot_general x24, matrix products, contract_cols(): lax.dot_general(left, right, (((1,), (1,)), ((), ())), preferred_element_...  88.8 us
    psum x1, waiting for transfers between devices, on_device(): lax.psum(matmul(attn_mixed, w_out), 'tensor') + out_bias.astype(jnp.float32)  80.7 us
    dot_general x18, matrix products, matmul(): return jnp.dot(left, right, preferred_element_type=jnp.float32)  77.6 us
    psum x1, blocking collectives, on_device(): lax.psum((w_query_grad, query_bias_grad, w_key_grad, w_value_grad, value_...  65.9 us
    ppermute x16, waiting for transfers between devices, from_behind(): return lax.ppermute(block, axis, route)  65.3 us
    dot_general x18, matrix products, contract_rows(): lax.dot_general(left, right, (((0,), (0,)), ((), ())), preferred_element_...  62.4 us
    psum x1, waiting for transfers between devices, on_device(): mlp_in_grad = lax.psum(contract_cols(pre_grad, w_fc1), 'tensor')  47.4 us
  transfers between devices with their start and end apart: 21, of which 9 were waited for; matrix products, arithmetic and copies ran while one was open for 9% of the time, Pallas kernels for 0%

profile of v1, /device:TPU:0, one launch (start us, length us, event | category | flops | bytes accessed | tf_op | source)
XLA Modules:
  0.0 990.1 jit_solution(4125132774011656002)
XLA Ops:
  13.6 5.7 collective-permute-start.4
  25.7 6.1 collective-permute-start
  42.5 8.9 collective-permute-done.4
  70.8 6.5 copy.43
  93.4 6.5 copy.42
  100.7 99.6 %while.28 = (s32[]{:T(128)}, bf16[6,768,64]{1,2,0:T(8,128)(2,1)}, f32[6,768]{1,0:T(8,128)}, bf16[6,768,64]{2,1,0:T(8,128)(2,1)}, bf16[6,3840,64]{2,1,0:T(8,128)(...) while((s32[]{:T(128)}, bf16[6,768,64]{1,2,0:T(8,128)(2,1)}, ...), condition=%wide.region_5.6_spmd.clone, body=%wide.region_2.5_spmd.clone.sunk | while | flops 781565184 | bytes 84894856 | solution.py:119
  109.8 7.6 fusion.155
  126.3 7.6 fusion.155
  142.9 7.6 fusion.155
  159.5 7.6 fusion.155
  176.1 7.6 fusion.155
  192.7 7.6 fusion.155
  206.6 80.7 %all-reduce.7.cloned.1.call-done = f32[768,768]{1,0:T(8,128)} async-done(((f32[768,768]{1,0:T(8,128)}), f32[768,768]{1,0:T(8,128)}) %all-reduce.7.cloned.1.call-update) | async-done | bytes 2359312 | tf_op jit(solution)/shard_map/psum | solution.py:121
  294.2 14.3 %convert_reduce_fusion = (f32[1536]{0:T(1024)}, bf16[768,1536]{1,0:T(8,128)(2,1)S(1)}, f32[768,1536]{1,0:T(8,128)}) fusion(f32[768,1536]{1,0:T(8,128)S(1)} %fusion.82, f32[1536]{0:T(1024)S(1)} %copy-done.42, bf16[768,768]{1,0:T(8,128)(2,1)S(1)} %copy-done.15, bf16[1536,768]{1,0:T(8,128)(2,1)S(1)} %copy-done), kind=kOutput, calls=%fused_computation.56 | convolution fusion | flops 1900411392 | bytes 15347712 | tf_op jit(solution)/shard_map/dot_general | solution.py:38
  324.2 6.0 fusion.99
  334.8 47.4 %all-reduce.9.cloned.1.call-done = f32[768,768]{1,0:T(8,128)} async-done(((f32[768,768]{1,0:T(8,128)}), f32[768,768]{1,0:T(8,128)}) %all-reduce.9.cloned.1.call-update) | async-done | bytes 2359312 | tf_op jit(solution)/shard_map/psum | solution.py:141
  385.9 34.5 %all-gather.3.cloned.1.call-done = bf16[1536,768]{1,0:T(8,128)(2,1)} async-done(((bf16[768,768]{1,0:T(8,128)(2,1)}), bf16[1536,768]{1,0:T(8,128)(2,1)}) %all-gather.3.cloned.1.call-update) | async-done | bytes 2359312 | tf_op jit(solution)/shard_map/all_gather | solution.py:131
  430.8 137.7 %while.29 = (s32[]{:T(128)}, bf16[6,768,64]{1,2,0:T(8,128)(2,1)S(1)}, f32[6,3840,64]{1,2,0:T(8,128)}, f32[6,3840,64]{1,2,0:T(8,128)}, bf16[6,768,64]{2,1,0:T(8,1...) while((s32[]{:T(128)}, ...), condition=%wide.region_15.16_spmd.clone, body=%wide.region_13.15_spmd.clone.sunk | while | flops 1917271296 | bytes 117906576 | solution.py:162
  443.4 5.0 fusion.166
  466.4 5.0 fusion.166
  489.3 5.0 fusion.166
  512.3 5.0 fusion.166
  526.3 5.0 multiply_reduce_fusion.5
  535.2 5.0 fusion.166
  558.1 5.0 fusion.166
  568.5 5.1 bitcast_convert_fusion
  588.7 42.1 %collective-permute-done.11 = bf16[768,384]{0,1:T(8,128)(2,1)S(1)} collective-permute-done((bf16[768,384]{0,1:T(8,128)(2,1)S(1)}, bf16[768,384]{0,1:T(8,128)(2,1)S(1)}, u32[]{:S(2)}, u32[]{:S(2)}) %collective-permute-start.11) | collective-permute-done | bytes 589856 | tf_op jit(solution)/shard_map/ppermute | solution.py:13
  630.8 5.8 collective-permute-start.14
  642.0 12.5 %collective-permute-done.15 = bf16[768,384]{0,1:T(8,128)(2,1)S(1)} collective-permute-done((bf16[768,384]{0,1:T(8,128)(2,1)S(1)}, bf16[768,384]{0,1:T(8,128)(2,1)S(1)}, u32[]{:S(2)}, u32[]{:S(2)}) %collective-permute-start.15) | collective-permute-done | bytes 589856 | tf_op jit(solution)/shard_map/ppermute | solution.py:13
  667.1 36.1 %all-reduce.11.cloned.1.call-done = bf16[768,768]{1,0:T(8,128)(2,1)} async-done(((bf16[768,768]{1,0:T(8,128)(2,1)}), bf16[768,768]{1,0:T(8,128)(2,1)}) %all-reduce.11.cloned.1.call-update) | async-done | bytes 1179664 | tf_op jit(solution)/shard_map/psum | solution.py:200
  712.9 65.9 %all-reduce = (f32[768]{0:T(1024)}, f32[768]{0:T(1024)}, f32[384]{0:T(512)}, f32[384]{0:T(512)}, f32[768]{0:T(1024)}, /*index=5*/f32[768]{0:T(1024)}, f32[768]{0:T(1024)}, f32[1536]{0:T(1024)}, f32[768]{0:T(1024)}) all-reduce(f32[768]{0:T(1024)} %get-tuple-element.181, ...), channel_id=1, replica_groups=mesh['dp'=16,'tensor'=2] {'dp'}, use_global_device_ids=true, to_apply=%region_20.21 | all-reduce | flops 6912 | bytes 55296 | tf_op jit(solution)/shard_map/psum | solution.py:219
  778.9 192.2 %all-reduce.13.cloned.1.call-done = (f32[768,384]{1,0:T(8,128)}, f32[768,384]{1,0:T(8,128)}, f32[768,384]{1,0:T(8,128)}, f32[384,768]{1,0:T(8,128)}, f32[768,1536]{1,0:T(8,128)}, /*index=5*/f32[1536,768]{1,0:T(8,128)}) async-done(((f32[768,384]{1,0:T(8,128)}, f32[768,384]{1,0:T(8,128)}, f32[768,384]{1,0:T(8,128)}, f32[384,768]{1,0:T(8,128)}, f32[768,1536]{1,0:T(8,128)}, /*index=5*/f32[1536,768]{1,0:T(8,128)}), ...) | async-done | bytes 14155792 | tf_op jit(solution)/shard_map/psum | solution.py:219
  (319 shorter events, 318.2 us)
Async XLA Ops:
  7.2 286.9 %copy-start = (bf16[1536,768]{1,0:T(8,128)(2,1)S(1)}, bf16[1536,768]{1,0:T(8,128)(2,1)}, u32[]{:S(2)}) copy-start(bf16[1536,768]{1,0:T(8,128)(2,1)} %param.37) | copy-start | bytes 7077892
  7.2 280.1 %all-reduce.7.cloned.1.call-start = ((), (), s32[]{:S(2)}) async-start(), calls=%async_computation | async-start | bytes 4718592 | tf_op jit(solution)/shard_map/psum | solution.py:121
  11.9 19.9 %copy-start.10 = (bf16[768,768]{1,0:T(8,128)(2,1)}, bf16[768,768]{1,0:T(8,128)(2,1)S(1)}, u32[]{:S(2)}) copy-start(bf16[768,768]{1,0:T(8,128)(2,1)S(1)} %fusion.63) | copy-start | bytes 3538948
  12.0 19.9 %copy-start.50 = (bf16[384]{0:T(512)(128)(2,1)S(1)}, bf16[384]{0:T(512)(128)(2,1)}, u32[]{:S(2)}) copy-start(bf16[384]{0:T(512)(128)(2,1)} %param.27) | copy-start | bytes 2308
  12.0 19.9 %copy-start.27 = (bf16[768,384]{1,0:T(8,128)(2,1)S(1)}, bf16[768,384]{1,0:T(8,128)(2,1)}, u32[]{:S(2)}) copy-start(bf16[768,384]{1,0:T(8,128)(2,1)} %param.26) | copy-start | bytes 1769476
  13.6 37.8 %collective-permute-start.4 = (bf16[768,384]{1,0:T(8,128)(2,1)}, bf16[768,384]{1,0:T(8,128)(2,1)}, u32[]{:S(2)}, u32[]{:S(2)}) collective-permute-start(bf16[768,384]{1,0:T(8,128)(2,1)} %fusion.70), channel_id=1, source_target_pairs={{0,4},{2,6},{4,8},{6,10},{8,12},{10,14},{12,16},{14,18},{16,20},{1... | collective-permute-start | bytes 1769480 | tf_op jit(solution)/shard_map/ppermute | solution.py:13
  19.3 36.2 %collective-permute-start.5 = (bf16[768,384]{1,0:T(8,128)(2,1)}, bf16[768,384]{1,0:T(8,128)(2,1)}, u32[]{:S(2)}, u32[]{:S(2)}) collective-permute-start(bf16[768,384]{1,0:T(8,128)(2,1)} %fusion.70), channel_id=1, source_target_pairs={{0,2},{2,4},{4,6},{6,8},{8,10},{10,12},{12,14},{14,16},{16,18},{18... | collective-permute-start | bytes 1769480 | tf_op jit(solution)/shard_map/ppermute | solution.py:13
  21.5 39.1 %collective-permute-start.6 = (bf16[768,384]{1,0:T(8,128)(2,1)}, bf16[768,384]{1,0:T(8,128)(2,1)}, u32[]{:S(2)}, u32[]{:S(2)}) collective-permute-start(bf16[768,384]{1,0:T(8,128)(2,1)} %fusion.70), channel_id=1, source_target_pairs={{2,0},{4,2},{6,4},{8,6},{10,8},{12,10},{14,12},{16,14},{18,16},{20... | collective-permute-start | bytes 1769480 | tf_op jit(solution)/shard_map/ppermute | solution.py:13
  22.8 41.6 %collective-permute-start.7 = (bf16[768,384]{1,0:T(8,128)(2,1)}, bf16[768,384]{1,0:T(8,128)(2,1)}, u32[]{:S(2)}, u32[]{:S(2)}) collective-permute-start(bf16[768,384]{1,0:T(8,128)(2,1)} %fusion.70), channel_id=1, source_target_pairs={{4,0},{6,2},{8,4},{10,6},{12,8},{14,10},{16,12},{18,14},{20,16},{2... | collective-permute-start | bytes 1769480 | tf_op jit(solution)/shard_map/ppermute | solution.py:13
  25.7 51.6 %collective-permute-start = (bf16[768,384]{1,0:T(8,128)(2,1)}, bf16[768,384]{1,0:T(8,128)(2,1)}, u32[]{:S(2)}, u32[]{:S(2)}) collective-permute-start(bf16[768,384]{1,0:T(8,128)(2,1)} %convolution_convert_fusion.2), channel_id=1, source_target_pairs={{0,4},{2,6},{4,8},{6,10},{8,12},{10,14},{12,16},{14,18},{16,20},{1... | collective-permute-start | bytes 1769480 | tf_op jit(solution)/shard_map/ppermute | solution.py:13
  51.4 27.9 %collective-permute-start.1 = (bf16[768,384]{1,0:T(8,128)(2,1)}, bf16[768,384]{1,0:T(8,128)(2,1)}, u32[]{:S(2)}, u32[]{:S(2)}) collective-permute-start(bf16[768,384]{1,0:T(8,128)(2,1)} %convolution_convert_fusion.2), channel_id=1, source_target_pairs={{0,2},{2,4},{4,6},{6,8},{8,10},{10,12},{12,14},{14,16},{16,18},{18... | collective-permute-start | bytes 1769480 | tf_op jit(solution)/shard_map/ppermute | solution.py:13
  55.5 27.7 %collective-permute-start.2 = (bf16[768,384]{1,0:T(8,128)(2,1)}, bf16[768,384]{1,0:T(8,128)(2,1)}, u32[]{:S(2)}, u32[]{:S(2)}) collective-permute-start(bf16[768,384]{1,0:T(8,128)(2,1)} %convolution_convert_fusion.2), channel_id=1, source_target_pairs={{2,0},{4,2},{6,4},{8,6},{10,8},{12,10},{14,12},{16,14},{18,16},{20... | collective-permute-start | bytes 1769480 | tf_op jit(solution)/shard_map/ppermute | solution.py:13
  60.6 26.3 %collective-permute-start.3 = (bf16[768,384]{1,0:T(8,128)(2,1)}, bf16[768,384]{1,0:T(8,128)(2,1)}, u32[]{:S(2)}, u32[]{:S(2)}) collective-permute-start(bf16[768,384]{1,0:T(8,128)(2,1)} %convolution_convert_fusion.2), channel_id=1, source_target_pairs={{4,0},{6,2},{8,4},{10,6},{12,8},{14,10},{16,12},{18,14},{20,16},{2... | collective-permute-start | bytes 1769480 | tf_op jit(solution)/shard_map/ppermute | solution.py:13
  203.8 178.3 %all-reduce.9.cloned.1.call-start = ((), (), s32[]{:S(2)}) async-start(), calls=%async_computation.1 | async-start | bytes 4718592 | tf_op jit(solution)/shard_map/psum | solution.py:141
  313.4 107.0 %all-gather.3.cloned.1.call-start = ((), (), s32[]{:S(2)}) async-start(), calls=%async_computation.3 | async-start | bytes 3538944 | tf_op jit(solution)/shard_map/all_gather | solution.py:131
  322.8 380.4 %all-reduce.11.cloned.1.call-start = ((), (), s32[]{:S(2)}) async-start(), calls=%async_computation.2 | async-start | bytes 2359296 | tf_op jit(solution)/shard_map/psum | solution.py:200
  573.8 13.4 %collective-permute-start.10 = (bf16[768,384]{0,1:T(8,128)(2,1)S(1)}, bf16[768,384]{0,1:T(8,128)(2,1)S(1)}, u32[]{:S(2)}, u32[]{:S(2)}) collective-permute-start(bf16[768,384]{0,1:T(8,128)(2,1)S(1)} %bitcast.190), channel_id=1, source_target_pairs={{0,2},{2,4},{4,6},{6,8},{8,10},{10,12},{12,14},{14,16},{16,18},{18... | collective-permute-start | bytes 1769480 | tf_op jit(solution)/shard_map/ppermute | solution.py:13
  575.6 55.2 %collective-permute-start.11 = (bf16[768,384]{0,1:T(8,128)(2,1)S(1)}, bf16[768,384]{0,1:T(8,128)(2,1)S(1)}, u32[]{:S(2)}, u32[]{:S(2)}) collective-permute-start(bf16[768,384]{0,1:T(8,128)(2,1)S(1)} %bitcast.189), channel_id=1, source_target_pairs={{0,4},{2,6},{4,8},{6,10},{8,12},{10,14},{12,16},{14,18},{16,20},{1... | collective-permute-start | bytes 1769480 | tf_op jit(solution)/shard_map/ppermute | solution.py:13
  579.2 57.5 %collective-permute-start.8 = (bf16[768,384]{0,1:T(8,128)(2,1)S(1)}, bf16[768,384]{0,1:T(8,128)(2,1)S(1)}, u32[]{:S(2)}, u32[]{:S(2)}) collective-permute-start(bf16[768,384]{0,1:T(8,128)(2,1)S(1)} %bitcast.187), channel_id=1, source_target_pairs={{4,0},{6,2},{8,4},{10,6},{12,8},{14,10},{16,12},{18,14},{20,16},{2... | collective-permute-start | bytes 1769480 | tf_op jit(solution)/shard_map/ppermute | solution.py:13
  580.5 60.3 %collective-permute-start.9 = (bf16[768,384]{0,1:T(8,128)(2,1)S(1)}, bf16[768,384]{0,1:T(8,128)(2,1)S(1)}, u32[]{:S(2)}, u32[]{:S(2)}) collective-permute-start(bf16[768,384]{0,1:T(8,128)(2,1)S(1)} %bitcast.183), channel_id=1, source_target_pairs={{2,0},{4,2},{6,4},{8,6},{10,8},{12,10},{14,12},{16,14},{18,16},{20... | collective-permute-start | bytes 1769480 | tf_op jit(solution)/shard_map/ppermute | solution.py:13
  582.1 59.9 %collective-permute-start.12 = (bf16[768,384]{0,1:T(8,128)(2,1)S(1)}, bf16[768,384]{0,1:T(8,128)(2,1)S(1)}, u32[]{:S(2)}, u32[]{:S(2)}) collective-permute-start(bf16[768,384]{0,1:T(8,128)(2,1)S(1)} %bitcast.188), channel_id=1, source_target_pairs={{4,0},{6,2},{8,4},{10,6},{12,8},{14,10},{16,12},{18,14},{20,16},{2... | collective-permute-start | bytes 1769480 | tf_op jit(solution)/shard_map/ppermute | solution.py:13
  587.2 53.9 %copy-start.30 = (bf16[768,384]{1,0:T(8,128)(2,1)S(1)}, bf16[768,384]{1,0:T(8,128)(2,1)}, u32[]{:S(2)}) copy-start(bf16[768,384]{1,0:T(8,128)(2,1)} %param.28) | copy-start | bytes 1769476
  587.3 54.7 %collective-permute-start.13 = (bf16[768,384]{0,1:T(8,128)(2,1)S(1)}, bf16[768,384]{0,1:T(8,128)(2,1)S(1)}, u32[]{:S(2)}, u32[]{:S(2)}) collective-permute-start(bf16[768,384]{0,1:T(8,128)(2,1)S(1)} %bitcast.186), channel_id=1, source_target_pairs={{2,0},{4,2},{6,4},{8,6},{10,8},{12,10},{14,12},{16,14},{18,16},{20... | collective-permute-start | bytes 1769480 | tf_op jit(solution)/shard_map/ppermute | solution.py:13
  630.8 11.2 %collective-permute-start.14 = (bf16[768,384]{0,1:T(8,128)(2,1)S(1)}, bf16[768,384]{0,1:T(8,128)(2,1)S(1)}, u32[]{:S(2)}, u32[]{:S(2)}) collective-permute-start(bf16[768,384]{0,1:T(8,128)(2,1)S(1)} %bitcast.185), channel_id=1, source_target_pairs={{0,2},{2,4},{4,6},{6,8},{8,10},{10,12},{12,14},{14,16},{16,18},{18... | collective-permute-start | bytes 1769480 | tf_op jit(solution)/shard_map/ppermute | solution.py:13
  636.6 17.8 %collective-permute-start.15 = (bf16[768,384]{0,1:T(8,128)(2,1)S(1)}, bf16[768,384]{0,1:T(8,128)(2,1)S(1)}, u32[]{:S(2)}, u32[]{:S(2)}) collective-permute-start(bf16[768,384]{0,1:T(8,128)(2,1)S(1)} %bitcast.184), channel_id=1, source_target_pairs={{0,4},{2,6},{4,8},{6,10},{8,12},{10,14},{12,16},{14,18},{16,20},{1... | collective-permute-start | bytes 1769480 | tf_op jit(solution)/shard_map/ppermute | solution.py:13
  657.5 313.6 %all-reduce.13.cloned.1.call-start = ((), (), s32[]{:S(2)}) async-start(), calls=%async_computation.4 | async-start | bytes 28311552 | tf_op jit(solution)/shard_map/psum | solution.py:219
  666.2 37.0 %copy-start.5 = (bf16[768,768]{1,0:T(8,128)(2,1)S(1)}, bf16[768,768]{1,0:T(8,128)(2,1)}, u32[]{:S(2)}) copy-start(bf16[768,768]{1,0:T(8,128)(2,1)} %param.22) | copy-start | bytes 3538948
  666.2 37.0 %copy-start.32 = (f32[768]{0:T(1024)S(1)}, f32[768]{0:T(1024)}, u32[]{:S(2)}) copy-start(f32[768]{0:T(1024)} %copy-done.31) | copy-start | bytes 9220
  666.2 37.0 %copy-start.34 = (f32[768]{0:T(1024)S(1)}, f32[768]{0:T(1024)}, u32[]{:S(2)}) copy-start(f32[768]{0:T(1024)} %copy-done.33) | copy-start | bytes 9220
  666.3 40.5 %copy-start.36 = (f32[768]{0:T(1024)S(1)}, f32[768]{0:T(1024)}, u32[]{:S(2)}) copy-start(f32[768]{0:T(1024)} %copy-done.35) | copy-start | bytes 9220
  667.1 42.9 %copy-start.16 = (bf16[768,768]{1,0:T(8,128)(2,1)S(1)}, bf16[768,768]{1,0:T(8,128)(2,1)}, u32[]{:S(2)}) copy-start(bf16[768,768]{1,0:T(8,128)(2,1)} %param.39) | copy-start | bytes 3538948
  667.1 42.9 %copy-start.38 = (f32[768]{0:T(1024)S(1)}, f32[768]{0:T(1024)}, u32[]{:S(2)}) copy-start(f32[768]{0:T(1024)} %copy-done.37) | copy-start | bytes 9220
  (55 other events, 227.8 us)
Sparse Core Ops, SparseCore 0:
  203.9 83.3 all-reduce.6
  313.5 68.6 all-reduce.8
  384.3 36.0 all-gather.2
  657.6 45.5 all-reduce.10
  710.2 260.9 all-reduce.12
